TPU v7x, 256 devices: a whole 4x4x8 slice. The times are simulated.
256 devices in a mesh: group: 64 (over y, z, core), mp: 4 (over x).
Axes of the slice: x: 4, y: 4, z: 8, core: 2. Of those that a mesh axis runs over, the one named last changes fastest.
Arguments:
- database: bfloat16 [384, 128, 4096], P('group', 'mp'), may hold values from -6 to 6
- head_weight: bfloat16 [4096, 2048], P(None, 'mp'), may hold values from -0.09375 to 0.09375
- value_weight: bfloat16 [4096, 2048], P(None, 'mp'), may hold values from -0.09375 to 0.09375
- segment_query: bfloat16 [53248, 2048], P('group', 'mp'), may hold values from -90 to 90
- segment_key: bfloat16 [53248, 2048], P('group', 'mp'), may hold values from -90 to 90
- segment_value: bfloat16 [53248, 2048], P('group', 'mp'), may hold values from -6 to 6
- owner_shard: int32 [832, 2], P('group'), may hold values from 0 to 63, as said below
- entry_slot: int32 [832, 2], P('group'), may hold values from 0 to 5
Outputs:
- attended: bfloat16 [53248, 2048], P('group', 'mp')
Inputs may be any that keep to these rules, and one draw needn't show every extreme that they name: `owner_shard`: among the rows of one index of group no shard is named more than 1 times, and one shard is named exactly 1 times by the rows of every index.
All inputs are finite; a program needn't handle non-finite values.
Results may differ from a plain program's by a relative error of at most 0.025.
The roundings to bfloat16 on the way count: a program that leaves them out, or rounds other values in their place, can miss the bound.
Values may be sent and summed in bfloat16 or wider, within the bound.
No kernel may reach another device: no remote copies, remote signals or barrier semaphores. Data moves between devices by JAX's collectives and lax.ppermute only.
A program may use at most 128 MiB of HBM per device.

v0:
```python
import jax
import jax.numpy as jnp
from jax import lax
from jax.sharding import PartitionSpec as P

HEAD_DIM = 128


def partial_attend(neighbour_rows, queries, segment_keys, segment_values):
    leading = neighbour_rows.shape[:-2]
    length = neighbour_rows.shape[-2]
    inner_width = neighbour_rows.shape[-1] // 2
    n_heads = inner_width // HEAD_DIM
    seg_len = queries.shape[-2]
    factor = HEAD_DIM ** (-0.5)
    head_rows = neighbour_rows[..., :inner_width].reshape(leading + (length, n_heads, HEAD_DIM))
    value_matrix_rows = neighbour_rows[..., inner_width:].reshape(
        leading + (length, n_heads, HEAD_DIM)
    )
    query_heads = queries.reshape(leading + (seg_len, n_heads, HEAD_DIM))
    key_heads = segment_keys.reshape(leading + (seg_len, n_heads, HEAD_DIM))
    value_heads = segment_values.reshape(leading + (seg_len, n_heads, HEAD_DIM))
    scores = (
        jnp.einsum(
            "...nhd,...thd->...hnt", head_rows, key_heads, preferred_element_type=jnp.float32
        )
        * factor
    )
    weights = jax.nn.softmax(scores, axis=-1).astype(jnp.bfloat16)
    encoded = (
        head_rows.astype(jnp.float32)
        + jnp.einsum(
            "...hnt,...thd->...nhd", weights, value_heads, preferred_element_type=jnp.float32
        )
    ).astype(jnp.bfloat16)
    cross = (
        jnp.einsum(
            "...thd,...nhd->...htn", query_heads, encoded, preferred_element_type=jnp.float32
        )
        * factor
    )
    highest = jnp.max(cross, axis=-1)
    exponent = jnp.exp(cross - highest[..., None])
    totals = jnp.sum(exponent, axis=-1)
    numerator = jnp.einsum(
        "...htn,...nhd->...thd",
        exponent,
        value_matrix_rows.astype(jnp.float32),
        precision=lax.Precision.HIGHEST,
    )
    return (numerator, highest, totals)


def per_device(
    database,
    head_weight,
    value_weight,
    segment_query,
    segment_key,
    segment_value,
    owner_shard,
    entry_slot,
):
    owners = lax.axis_size("group")
    inner_width = head_weight.shape[1]
    seg_dev = owner_shard.shape[0]
    neigh_count = owner_shard.shape[1]
    seg_len = segment_query.shape[0] // seg_dev
    requests = seg_dev * neigh_count
    capacity = max(1, (requests + owners - 1) // owners)
    slot_count = owners * capacity
    both_weights = jnp.concatenate([head_weight, value_weight], axis=1)
    projected = jnp.einsum(
        "erx,xc->erc",
        lax.all_gather(database, "mp", axis=1, tiled=True),
        both_weights,
        preferred_element_type=jnp.float32,
    ).astype(jnp.bfloat16)
    request_owner = owner_shard.reshape(requests)
    request_entry = entry_slot.reshape(requests)
    request_ids = jnp.arange(requests, dtype=jnp.int32)
    earlier = (request_owner[:, None] == request_owner[None, :]) & (
        request_ids[None, :] < request_ids[:, None]
    )
    slot_of = request_owner * capacity + jnp.sum(earlier, axis=1)
    matches = slot_of[None, :] == jnp.arange(slot_count, dtype=jnp.int32)[:, None]
    request_at = jnp.sum(jnp.where(matches, request_ids[None, :], 0), axis=1)
    occupied = jnp.any(matches, axis=1)
    entry_at = jnp.where(occupied, request_entry[request_at], 0).reshape(owners, capacity)
    queries = segment_query.reshape(seg_dev, seg_len, inner_width)
    seg_keys = segment_key.reshape(seg_dev, seg_len, inner_width)
    seg_values = segment_value.reshape(seg_dev, seg_len, inner_width)
    segment_at = request_at // neigh_count
    block_shape = (owners, capacity, seg_len, inner_width)
    shares = partial_attend(
        projected[lax.all_to_all(entry_at, "group", split_axis=0, concat_axis=0, tiled=True)],
        lax.all_to_all(
            queries[segment_at].reshape(block_shape),
            "group",
            split_axis=0,
            concat_axis=0,
            tiled=True,
        ),
        lax.all_to_all(
            seg_keys[segment_at].reshape(block_shape),
            "group",
            split_axis=0,
            concat_axis=0,
            tiled=True,
        ),
        lax.all_to_all(
            seg_values[segment_at].reshape(block_shape),
            "group",
            split_axis=0,
            concat_axis=0,
            tiled=True,
        ),
    )
    returned = (
        lax.all_to_all(shares[0], "group", split_axis=0, concat_axis=0, tiled=True),
        lax.all_to_all(shares[1], "group", split_axis=0, concat_axis=0, tiled=True),
        lax.all_to_all(shares[2], "group", split_axis=0, concat_axis=0, tiled=True),
    )
    numerator = returned[0].reshape((slot_count,) + returned[0].shape[2:])[slot_of]
    highest = returned[1].reshape((slot_count,) + returned[1].shape[2:])[slot_of]
    totals = returned[2].reshape((slot_count,) + returned[2].shape[2:])[slot_of]
    numerator = numerator.reshape((seg_dev, neigh_count) + numerator.shape[1:])
    highest = highest.reshape((seg_dev, neigh_count) + highest.shape[1:])
    totals = totals.reshape((seg_dev, neigh_count) + totals.shape[1:])
    peak_value = jnp.max(highest, axis=1, keepdims=True)
    rescale = jnp.exp(highest - peak_value)
    denominator = jnp.sum(totals * rescale, axis=1)
    combined = jnp.sum(numerator * jnp.swapaxes(rescale, 2, 3)[..., None], axis=1)
    final_output = combined / jnp.swapaxes(denominator, 1, 2)[..., None]
    return final_output.reshape(seg_dev * seg_len, inner_width).astype(jnp.bfloat16)


def solution(mesh):
    in_specs = (
        P("group", "mp", None),
        P(None, "mp"),
        P(None, "mp"),
        P("group", "mp"),
        P("group", "mp"),
        P("group", "mp"),
        P("group", None),
        P("group", None),
    )
    out_specs = P("group", "mp")
    return jax.shard_map(
        per_device, mesh=mesh, in_specs=in_specs, out_specs=out_specs, check_vma=False
    )
```

profile of v0, /device:TPU:1, one launch (start us, length us, event | category | flops | bytes accessed | tf_op | source)
XLA Modules:
  0.0 656.6 jit_solution(17433418391482846126)
XLA Ops:
  10.2 13.2 %all-to-all-start = ((s32[64,1,1]{2,1,0:T(1,128)}), s32[64,1,1]{2,1,0:T(1,128)S(1)}, u32[]{:S(2)}, u32[]{:S(2)}) async-start(s32[64,1,1]{2,1,0:T(1,128)} %copy.59), calls=%async_computation | async-start | bytes 65536 | tf_op jit(solution)/shard_map/all_to_all | solution.py:96
  23.4 2.7 gather_fusion.4
  26.2 6.4 all-to-all-done
  32.6 5.7 all-to-all-start.3
  38.3 2.9 gather_fusion.3
  41.2 93.1 %all-to-all-done.3 = bf16[64,1,64,512]{3,2,1,0:T(8,128)(2,1)} async-done(((bf16[64,1,64,512]{3,2,1,0:T(8,128)(2,1)}), bf16[64,1,64,512]{3,2,1,0:T(8,128)(2,1)}, u32[]{:S(2)}, u32[]{:S(2)}) %all-to-all-start.3) | async-done | bytes 4194336 | tf_op jit(solution)/shard_map/all_to_all | solution.py:104
  134.2 6.0 all-to-all-start.2
  141.0 2.8 gather_fusion.2
  143.8 92.4 %all-to-all-done.2 = bf16[64,1,64,512]{3,2,1,0:T(8,128)(2,1)} async-done(((bf16[64,1,64,512]{3,2,1,0:T(8,128)(2,1)}), bf16[64,1,64,512]{3,2,1,0:T(8,128)(2,1)}, u32[]{:S(2)}, u32[]{:S(2)}) %all-to-all-start.2) | async-done | bytes 4194336 | tf_op jit(solution)/shard_map/all_to_all | solution.py:111
  236.1 5.9 all-to-all-start.1
  242.1 6.4 copy.56
  248.5 6.4 copy.55
  254.9 1.2 fusion.28
  256.1 6.9 %reshape.265 = bf16[64,64,4,128]{3,2,1,0:T(4,128)(2,1)} reshape(bf16[64,1,64,512]{3,2,1,0:T(8,128)(2,1)} %all-to-all-done.3) | data formatting | bytes 8388608 | tf_op jit(solution)/shard_map/reshape.1
  263.1 6.9 %reshape.261 = bf16[64,64,4,128]{3,2,1,0:T(4,128)(2,1)} reshape(bf16[64,1,64,512]{3,2,1,0:T(8,128)(2,1)} %all-to-all-done.2) | data formatting | bytes 8388608 | tf_op jit(solution)/shard_map/reshape.5
  270.0 67.9 %all-to-all-done.1 = bf16[64,1,64,512]{3,2,1,0:T(8,128)(2,1)} async-done(((bf16[64,1,64,512]{3,2,1,0:T(8,128)(2,1)}), bf16[64,1,64,512]{3,2,1,0:T(8,128)(2,1)}, u32[]{:S(2)}, u32[]{:S(2)}) %all-to-all-start.1) | async-done | bytes 4194336 | tf_op jit(solution)/shard_map/all_to_all | solution.py:97
  338.0 6.9 %reshape.258 = bf16[64,64,4,128]{3,2,1,0:T(4,128)(2,1)} reshape(bf16[64,1,64,512]{3,2,1,0:T(8,128)(2,1)} %all-to-all-done.1) | data formatting | bytes 8388608 | tf_op jit(solution)/shard_map/reshape.8
  344.9 9.9 %fusion.26 = bf16[6,128,1024]{1,2,0:T(8,128)(2,1)S(1)} fusion(bf16[6,128,4096]{2,1,0:T(8,128)(2,1)} %all-gather.2.cloned.1.call-done, bf16[4096,512]{0,1:T(8,128)(2,1)} %copy.56, bf16[4096,512]{0,1:T(8,128)(2,1)} %copy.55), kind=kOutput, calls=%fused_computation.37 | convolution fusion | flops 6460014592 | bytes 16252928 | tf_op jit(solution)/shard_map/erx,xc->erc/dot_general | solution.py:73
  354.8 7.2 %gather_fusion.1 = bf16[64,128,1024]{1,2,0:T(8,128)(2,1)} fusion(bf16[6,128,1024]{1,2,0:T(8,128)(2,1)S(1)} %fusion.26, s32[1024]{0:T(1024)S(1)} %pad_clamp_fusion.2), kind=kCustom, calls=%fused_computation.1 | custom fusion | bytes 33554688 | tf_op jit(solution)/shard_map/gather | solution.py:96
  362.1 9.4 %fusion.37 = (bf16[64,1,128,512]{2,3,0,1:T(8,128)(2,1)S(1)}, bf16[64,1,128,512]{2,3,0,1:T(8,128)(2,1)}) fusion(bf16[64,1,128,1024]{2,3,0,1:T(8,128)(2,1)} %bitcast.94), kind=kLoop, calls=%fused_computation.70 | loop fusion | bytes 33554432 | tf_op jit(solution)/shard_map/slice | solution.py:16
  372.1 2.3 fusion.14
  374.7 4.3 fusion.38
  379.0 13.4 %multiply_reduce_fusion = (f32[64,4,64]{2,1,0:T(4,128)S(1)}, f32[64,4,64,128]{3,2,1,0:T(8,128)}) fusion(f32[64,4,128,64]{2,3,1,0:T(8,128)} %get-tuple-element.12, f32[64,4,128]{2,1,0:T(4,128)S(1)} %get-tuple-element.11, bf16[64,64,4,128]{3,2,1,0:T(4,128)(2,1)} %reshape.261, bf16[64,1,128,4,128]{2,4,3,0,1:T(8,128)(2,1)} %bitcast.93, ...), kind=kOutput, calls=%fused_computation.20 | convolution fusion | flops 1094696960 | bytes 33751040 | tf_op jit(solution)/shard_map/...thd,...nhd->...htn/dot_general | solution.py:37
  392.4 7.1 %fusion.8 = f32[64,4,64]{2,1,0:T(4,128)S(1)} fusion(f32[64,4,64,128]{3,2,1,0:T(8,128)} %get-tuple-element.14, f32[64,4,64]{2,1,0:T(4,128)S(1)} %get-tuple-element.13), kind=kLoop, calls=%fused_computation.23 | loop fusion | flops 6275072 | bytes 8519680 | tf_op jit(solution)/shard_map/reduce_sum | solution.py:44
  400.3 6.1 all-to-all-start.6
  407.2 9.0 %all-to-all-done.6 = f32[64,1,256]{2,1,0:T(1,128)S(1)} async-done(((f32[64,1,256]{2,1,0:T(1,128)}), f32[64,1,256]{2,1,0:T(1,128)S(1)}, u32[]{:S(2)}, u32[]{:S(2)}) %all-to-all-start.6) | async-done | bytes 65568 | tf_op jit(solution)/shard_map/all_to_all | solution.py:122
  416.2 4.4 all-to-all-start.5
  420.5 21.9 %fusion.20 = f32[64,1,64,4,128]{4,2,3,1,0:T(8,128)} fusion(bf16[64,128,4,128]{1,3,2,0:T(8,128)(2,1)} %bitcast.95, f32[64,4,64,128]{3,2,1,0:T(8,128)} %get-tuple-element.14, f32[64,4,64]{2,1,0:T(4,128)S(1)} %get-tuple-element.13), kind=kOutput, calls=%fused_computation.34 | convolution fusion | flops 3225419776 | bytes 25231360 | tf_op jit(solution)/shard_map/...htn,...nhd->...thd/dot_general | solution.py:45
  442.4 10.6 %all-to-all-start.4 = ((f32[64,1,64,4,128]{4,2,3,1,0:T(8,128)}), f32[64,1,64,4,128]{4,2,3,1,0:T(8,128)}, u32[]{:S(2)}, u32[]{:S(2)}) async-start(f32[64,1,64,4,128]{4,2,3,1,0:T(8,128)} %fusion.20), calls=%async_computation.4 | async-start | bytes 16777216 | tf_op jit(solution)/shard_map/all_to_all | solution.py:120
  456.8 182.0 %all-to-all-done.4 = f32[64,1,64,4,128]{4,2,3,1,0:T(8,128)} async-done(((f32[64,1,64,4,128]{4,2,3,1,0:T(8,128)}), f32[64,1,64,4,128]{4,2,3,1,0:T(8,128)}, u32[]{:S(2)}, u32[]{:S(2)}) %all-to-all-start.4) | async-done | bytes 8388640 | tf_op jit(solution)/shard_map/all_to_all | solution.py:120
  638.8 6.0 gather_fusion.5
  644.8 2.6 multiply_reduce_fusion.2
  (47 shorter events, 12.8 us)
Async XLA Ops:
  6.5 16.9 %copy-start = (bf16[832,512]{1,0:T(8,128)(2,1)S(1)}, bf16[832,512]{1,0:T(8,128)(2,1)}, u32[]{:S(2)}) copy-start(bf16[832,512]{1,0:T(8,128)(2,1)} %param.12) | copy-start | bytes 2555908
  10.2 22.4 %all-to-all-start = ((s32[64,1,1]{2,1,0:T(1,128)}), s32[64,1,1]{2,1,0:T(1,128)S(1)}, u32[]{:S(2)}, u32[]{:S(2)}) async-start(s32[64,1,1]{2,1,0:T(1,128)} %copy.59), calls=%async_computation | async-start | bytes 65536 | tf_op jit(solution)/shard_map/all_to_all | solution.py:96
  23.4 14.9 %copy-start.4 = (bf16[832,512]{1,0:T(8,128)(2,1)S(1)}, bf16[832,512]{1,0:T(8,128)(2,1)}, u32[]{:S(2)}) copy-start(bf16[832,512]{1,0:T(8,128)(2,1)} %param.13) | copy-start | bytes 2555908
  32.6 101.6 %all-to-all-start.3 = ((bf16[64,1,64,512]{3,2,1,0:T(8,128)(2,1)}), bf16[64,1,64,512]{3,2,1,0:T(8,128)(2,1)}, u32[]{:S(2)}, u32[]{:S(2)}) async-start(bf16[64,1,64,512]{3,2,1,0:T(8,128)(2,1)} %bitcast.100), calls=%async_computation.3 | async-start | bytes 8388608 | tf_op jit(solution)/shard_map/all_to_all | solution.py:104
  38.3 102.7 %copy-start.5 = (bf16[832,512]{1,0:T(8,128)(2,1)S(1)}, bf16[832,512]{1,0:T(8,128)(2,1)}, u32[]{:S(2)}) copy-start(bf16[832,512]{1,0:T(8,128)(2,1)} %param.11) | copy-start | bytes 2555908
  134.2 101.9 %all-to-all-start.2 = ((bf16[64,1,64,512]{3,2,1,0:T(8,128)(2,1)}), bf16[64,1,64,512]{3,2,1,0:T(8,128)(2,1)}, u32[]{:S(2)}, u32[]{:S(2)}) async-start(bf16[64,1,64,512]{3,2,1,0:T(8,128)(2,1)} %bitcast.99), calls=%async_computation.2 | async-start | bytes 8388608 | tf_op jit(solution)/shard_map/all_to_all | solution.py:111
  140.2 204.6 %all-gather.2.cloned.1.call-start = ((), (), s32[]{:S(2)}) async-start(), calls=%async_computation.7 | async-start | bytes 7864320 | tf_op jit(solution)/shard_map/all_gather | solution.py:75
  236.1 101.8 %all-to-all-start.1 = ((bf16[64,1,64,512]{3,2,1,0:T(8,128)(2,1)}), bf16[64,1,64,512]{3,2,1,0:T(8,128)(2,1)}, u32[]{:S(2)}, u32[]{:S(2)}) async-start(bf16[64,1,64,512]{3,2,1,0:T(8,128)(2,1)} %bitcast.98), calls=%async_computation.1 | async-start | bytes 8388608 | tf_op jit(solution)/shard_map/all_to_all | solution.py:97
  362.1 10.0 %copy-start.3 = (bf16[64,64,4,128]{3,2,1,0:T(4,128)(2,1)S(1)}, bf16[64,64,4,128]{3,2,1,0:T(4,128)(2,1)}, u32[]{:S(2)}) copy-start(bf16[64,64,4,128]{3,2,1,0:T(4,128)(2,1)} %reshape.265) | copy-start | bytes 12582916
  371.5 3.2 copy-start.2
  400.3 15.9 %all-to-all-start.6 = ((f32[64,1,256]{2,1,0:T(1,128)}), f32[64,1,256]{2,1,0:T(1,128)S(1)}, u32[]{:S(2)}, u32[]{:S(2)}) async-start(f32[64,1,256]{2,1,0:T(1,128)} %reshape.343), calls=%async_computation.6 | async-start | bytes 131072 | tf_op jit(solution)/shard_map/all_to_all | solution.py:122
  416.2 26.2 %all-to-all-start.5 = ((f32[64,1,256]{2,1,0:T(1,128)}), f32[64,1,256]{2,1,0:T(1,128)S(1)}, u32[]{:S(2)}, u32[]{:S(2)}) async-start(f32[64,1,256]{2,1,0:T(1,128)} %reshape.341), calls=%async_computation.5 | async-start | bytes 131072 | tf_op jit(solution)/shard_map/all_to_all | solution.py:121
  442.4 196.4 %all-to-all-start.4 = ((f32[64,1,64,4,128]{4,2,3,1,0:T(8,128)}), f32[64,1,64,4,128]{4,2,3,1,0:T(8,128)}, u32[]{:S(2)}, u32[]{:S(2)}) async-start(f32[64,1,64,4,128]{4,2,3,1,0:T(8,128)} %fusion.20), calls=%async_computation.4 | async-start | bytes 16777216 | tf_op jit(solution)/shard_map/all_to_all | solution.py:120
  638.8 10.9 %copy-start.1 = (bf16[832,512]{1,0:T(8,128)(2,1)S(1)}, bf16[832,512]{1,0:T(8,128)(2,1)}, u32[]{:S(2)}) copy-start(bf16[832,512]{1,0:T(8,128)(2,1)} %param.12) | copy-start | bytes 2555908
Sparse Core Ops, SparseCore 0:
  142.9 69.1 all-gather.1
where the time goes:
time: 658 us; the launch traced here: 657 us
  waiting for transfers between devices  452 us (69%)
  local copies, waits for them, and re-layouts  74.1 us (11%)
  starting transfers between devices  51.9 us (8%)
  matrix products  47.6 us (7%)
  other arithmetic  17.9 us (3%)
  between operations  13.6 us (2%)
    all_to_all x1, waiting for transfers between devices, per_device(): lax.all_to_all(shares[0], 'group', split_axis=0, concat_axis=0, tiled=True)  182 us
    all_to_all x1, waiting for transfers between devices, per_device(): lax.all_to_all(seg_keys[segment_at].reshape(block_shape), 'group', split_...  93.1 us
    all_to_all x1, waiting for transfers between devices, per_device(): lax.all_to_all(seg_values[segment_at].reshape(block_shape), 'group', spli...  92.4 us
    all_to_all x1, waiting for transfers between devices, per_device(): lax.all_to_all(queries[segment_at].reshape(block_shape), 'group', split_a...  67.9 us
    dot_general x1, matrix products, partial_attend(): jnp.einsum('...htn,...nhd->...thd', exponent, value_matrix_rows.astype(jn...  21.9 us
    another operation x3, local copies, waits for them, and re-layouts  20.8 us
    unnamed x21, local copies, waits for them, and re-layouts  18.2 us
    dot_general x1, matrix products, partial_attend(): jnp.einsum('...thd,...nhd->...htn', query_heads, encoded, preferred_eleme...  13.4 us
  transfers between devices with their start and end apart: 8, of which 6 were waited for; matrix products, arithmetic and copies ran while one was open for 11% of the time, Pallas kernels for 0%

commit v1 on v0

v1 whole, which is shorter than its diff:
```python
import functools

import jax
import jax.numpy as jnp
from jax import lax
from jax.experimental import pallas as pl
from jax.experimental.pallas import tpu as pltpu
from jax.sharding import Mesh
from jax.sharding import PartitionSpec as P

HEAD_DIM = 128
NY, NZ, NC = 4, 8, 2
PLANE = NY * NC
DELTAS = (0, 7, 1, 6, 2, 5, 3, 4)
CHUNKS = ((0, 1, 2), (3, 4), (5, 6), (7,))
STAT = 128
LANES = 16
PAIR = 2


def project_kernel(parts, hw, vw, out, *scratch):
    rows_in, hbuf, vbuf, acc, in_sem, sem = (scratch[:-5], *scratch[-5:])
    entries, _, width = out.shape
    width //= 2
    steps, depth, _ = hbuf.shape
    loads = [pltpu.make_async_copy(p, r, in_sem.at[i]) for i, (p, r) in enumerate(zip(parts, rows_in))]
    weights = [
        [
            pltpu.make_async_copy(w.at[pl.ds(k * depth, depth)], buf.at[k], sem.at[i, k])
            for i, (w, buf) in enumerate(((hw, hbuf), (vw, vbuf)))
        ]
        for k in range(steps)
    ]
    for copy in loads:
        copy.start()
    for pair in weights:
        for copy in pair:
            copy.start()
    for copy in loads:
        copy.wait()
    for k in range(steps):
        for copy in weights[k]:
            copy.wait()
        row = 0
        for r in rows_in:
            count = entries * r.shape[1]
            x = r[:, :, k * depth : (k + 1) * depth].reshape(count, depth)
            for side, buf in ((0, hbuf), (1, vbuf)):
                span = (slice(row, row + count), slice(side * width, (side + 1) * width))
                y = jnp.dot(x, buf[k], preferred_element_type=jnp.float32)
                acc[span] = y if k == 0 else acc[span] + y
            row += count
    row = at = 0
    for r in rows_in:
        rows = r.shape[1]
        block = acc[row : row + entries * rows, :].astype(out.dtype)
        out[:, at : at + rows, :] = block.reshape(entries, rows, 2 * width)
        row += entries * rows
        at += rows


def project(parts, head_weight, value_weight):
    entries, _, depth = parts[0].shape
    rows = sum(p.shape[1] for p in parts)
    width = head_weight.shape[1]
    steps = 8
    n = len(parts)

    def kernel(*refs):
        project_kernel(refs[:n], *refs[n:])

    chunk = pltpu.VMEM((steps, depth // steps, width), jnp.bfloat16)
    return pl.pallas_call(
        kernel,
        in_specs=[pl.BlockSpec(memory_space=pl.ANY)] * (n + 2),
        out_specs=pl.BlockSpec(memory_space=pltpu.VMEM),
        out_shape=jax.ShapeDtypeStruct((entries, rows, 2 * width), jnp.bfloat16),
        scratch_shapes=[pltpu.VMEM(p.shape, p.dtype) for p in parts]
        + [
            chunk,
            chunk,
            pltpu.VMEM((entries * rows, 2 * width), jnp.float32),
            pltpu.SemaphoreType.DMA((n,)),
            pltpu.SemaphoreType.DMA((2, steps)),
        ],
        compiler_params=pltpu.CompilerParams(vmem_limit_bytes=60 << 20),
        cost_estimate=pl.CostEstimate(
            flops=4 * entries * rows * depth * width,
            bytes_accessed=4 * depth * width + 2 * entries * rows * (depth + 2 * width),
            transcendentals=0,
        ),
        name="project",
    )(*parts, head_weight, value_weight)


def matmul(a, b, da, db):
    return lax.dot_general(
        a, b, (((da,), (db,)), ((), ())), preferred_element_type=jnp.float32
    )


def attend_kernel(slots, counts, seg_at, entry_at, used_at, *refs):
    refs = list(refs)
    out = refs.pop()
    qkvs = [[refs.pop(0) for _ in range(PAIR)] for _ in slots]
    held = [[[refs.pop(0) for _ in range(PAIR)] for _ in range(n)] for n in counts]
    seg_len, width = out.shape[1], qkvs[0][0].shape[2] // 3
    factor = HEAD_DIM**-0.5
    lanes = lax.broadcasted_iota(jnp.int32, (seg_len, STAT), 1)
    units = [(s, h) for s in range(PAIR) for h in range(width // HEAD_DIM)]

    def part(ref, index, h):
        begin = index * width + h * HEAD_DIM
        return ref[0, :, begin : begin + HEAD_DIM]

    def run(place, qkv, pieces):
        def rows_of(s, index, h):
            return jnp.concatenate([part(p[s], index, h) for p in pieces], axis=0)

        states = [rows_of(s, 0, h) for s, h in units]
        scores = [
            matmul(part(qkv[s], 1, h), x, 1, 1) * factor for (s, h), x in zip(units, states)
        ]
        peaks = [jnp.max(x, axis=0, keepdims=True) for x in scores]
        scores = [jnp.exp(x - m) for x, m in zip(scores, peaks)]
        weights = [
            (x * (1.0 / jnp.sum(x, axis=0, keepdims=True))).astype(jnp.bfloat16) for x in scores
        ]
        encoded = [
            (x.astype(jnp.float32) + matmul(w, part(qkv[s], 2, h), 0, 0)).astype(jnp.bfloat16)
            for (s, h), x, w in zip(units, states, weights)
        ]
        cross = [
            matmul(part(qkv[s], 0, h), x, 1, 1) * factor for (s, h), x in zip(units, encoded)
        ]
        highest = [jnp.max(x, axis=1, keepdims=True) for x in cross]
        mix = [jnp.exp(x - m) for x, m in zip(cross, highest)]
        totals = [jnp.sum(x, axis=1, keepdims=True) for x in mix]
        shares = []
        for (s, h), x in zip(units, mix):
            upper = x.astype(jnp.bfloat16)
            lower = (x - upper.astype(jnp.float32)).astype(jnp.bfloat16)
            both = matmul(jnp.concatenate([upper, lower], axis=0), rows_of(s, 1, h), 1, 0)
            shares.append(both[:seg_len] + both[seg_len:])
        stats = [out[s, :, len(slots) * width :].astype(jnp.float32) for s in range(PAIR)]
        for (s, h), share, total, high in zip(units, shares, totals, highest):
            begin = place * width + h * HEAD_DIM
            out[s, :, begin : begin + HEAD_DIM] = (share * (1.0 / total)).astype(out.dtype)
            rest = high + jnp.log(total)
            for j in range(3):
                term = rest.astype(jnp.bfloat16).astype(jnp.float32)
                stats[s] = jnp.where(lanes == place * LANES + 3 * h + j, term, stats[s])
                rest = rest - term
        for s in range(PAIR):
            out[s, :, len(slots) * width :] = stats[s].astype(out.dtype)

    for place, (slot, qkv, pieces) in enumerate(zip(slots, qkvs, held)):
        at = slot * PLANE + pl.program_id(0) * PAIR
        used = used_at[at]
        for s in range(1, PAIR):
            used = used | used_at[at + s]
        pl.when(used != 0)(functools.partial(run, place, qkv, pieces))


def attend(slots, tables, qkv, held):
    segs, seg_len, width = qkv.shape
    width //= 3
    seg_dev = segs // PLANE

    def seg_spec(slot, s):
        def index(i, seg, entry, used):
            g = i * PAIR + s
            return g * seg_dev + seg[slot * PLANE + g], 0, 0

        return pl.BlockSpec((1, seg_len, 3 * width), index)

    def piece_spec(piece, slot, s):
        return pl.BlockSpec(
            (1,) + piece.shape[1:],
            lambda i, seg, entry, used: (entry[slot * PLANE + i * PAIR + s], 0, 0),
        )

    in_specs = [seg_spec(slot, s) for slot in slots for s in range(PAIR)]
    args = [*tables] + [qkv] * len(in_specs)
    for slot in slots:
        for piece in held[slot]:
            in_specs += [piece_spec(piece, slot, s) for s in range(PAIR)]
            args += [piece] * PAIR
    full = len(slots) * width + STAT
    return pl.pallas_call(
        functools.partial(attend_kernel, slots, [len(held[slot]) for slot in slots]),
        grid_spec=pltpu.PrefetchScalarGridSpec(
            num_scalar_prefetch=3,
            grid=(PLANE // PAIR,),
            in_specs=in_specs,
            out_specs=pl.BlockSpec((PAIR, seg_len, full), lambda i, *_: (i, 0, 0)),
        ),
        out_shape=jax.ShapeDtypeStruct((PLANE, seg_len, full), jnp.bfloat16),
        compiler_params=pltpu.CompilerParams(vmem_limit_bytes=60 << 20),
        cost_estimate=pl.CostEstimate(flops=1 << 20, bytes_accessed=1 << 20, transcendentals=0),
        name="attend",
    )(*args)


def combine_kernel(src, slot, *refs):
    backs, out = refs[:-1], refs[-1]
    seg_len = backs[0].shape[1]
    width = out.shape[1]

    def part(i, begin, size, per_place):
        value = None
        for slots, back in zip(CHUNKS, backs):
            here = (slot[i] >= slots[0]) & (slot[i] <= slots[-1])
            offset = jnp.where(here, slot[i] - slots[0], 0) * per_place + begin(len(slots))
            block = back[src[i], :, pl.ds(pl.multiple_of(offset, 128), size)]
            value = block if value is None else jnp.where(here, block, value)
        return value.astype(jnp.float32)

    def total(i):
        first = 0
        for slots in CHUNKS:
            here = (slot[i] >= slots[0]) & (slot[i] <= slots[-1])
            first = jnp.where(here, (slot[i] - slots[0]) * LANES, first)
        x = part(i, lambda n: n * width, STAT, 0)
        x = pltpu.roll(x, STAT - first, 1)
        return x + pltpu.roll(x, STAT - 1, 1) + pltpu.roll(x, STAT - 2, 1)

    @pl.loop(0, out.shape[0] // seg_len)
    def _(s):
        more = total(2 * s + 1) - total(2 * s)
        one = 1.0 / (1.0 + jnp.exp(more))
        two = 1.0 / (1.0 + jnp.exp(-more))
        rows = pl.ds(pl.multiple_of(s * seg_len, seg_len), seg_len)
        for h in range(width // HEAD_DIM):
            first = part(2 * s, lambda n: h * HEAD_DIM, HEAD_DIM, width)
            second = part(2 * s + 1, lambda n: h * HEAD_DIM, HEAD_DIM, width)
            lane = slice(3 * h, 3 * h + 1)
            out[rows, h * HEAD_DIM : (h + 1) * HEAD_DIM] = (
                first * one[:, lane] + second * two[:, lane]
            ).astype(out.dtype)


def combine(backs, src, slot):
    _, seg_len, full = backs[0].shape
    width = (full - STAT) // len(CHUNKS[0])
    return pl.pallas_call(
        combine_kernel,
        in_specs=[pl.BlockSpec(memory_space=pltpu.SMEM)] * 2
        + [pl.BlockSpec(memory_space=pltpu.VMEM)] * len(backs),
        out_specs=pl.BlockSpec(memory_space=pltpu.VMEM),
        out_shape=jax.ShapeDtypeStruct((src.shape[0] // 2 * seg_len, width), jnp.bfloat16),
        compiler_params=pltpu.CompilerParams(vmem_limit_bytes=60 << 20),
        name="combine",
    )(src, slot, *backs)


def hop(x, axis, step):
    n = lax.axis_size(axis)
    return lax.ppermute(x, axis, [(i, (i + step) % n) for i in range(n)])


def after(value, event):
    return lax.optimization_barrier((value, event))[0]


def ring(pieces, hops=NZ // 2):
    held = pieces if isinstance(pieces, list) else [[pieces]]
    while len(held) < min(2 * hops + 1, NZ):
        if len(held) < NZ - 1:
            forward, backward = held[-2:] if len(held) > 1 else held * 2
            held = held + [[hop(forward[0], "z", 1)], [hop(backward[0], "z", -1)]]
        else:
            (forward,), (backward,) = held[-2:]
            cut = forward.shape[1] // 2
            held = held + [[hop(forward[:, :cut], "z", 1), hop(backward[:, cut:], "z", -1)]]
    return held


def per_device(
    database,
    head_weight,
    value_weight,
    segment_query,
    segment_key,
    segment_value,
    owner_shard,
    entry_slot,
):
    entries, rows, _ = database.shape
    seg_dev = owner_shard.shape[0]
    seg_len = segment_query.shape[0] // seg_dev
    width = segment_query.shape[1]
    y, z, c = lax.axis_index("y"), lax.axis_index("z"), lax.axis_index("c")

    qkv = jnp.concatenate([segment_query, segment_key, segment_value], axis=1)
    qkv = lax.all_gather(qkv, ("y", "c"), axis=0, tiled=True).reshape(-1, seg_len, 3 * width)

    from_left, from_right = hop(database, "mp", 1), hop(database, "mp", -1)
    own = ring(project([database], head_weight, value_weight), 2)
    own[3:5], from_left, from_right = lax.optimization_barrier((own[3:5], from_left, from_right))
    half = rows // 2
    far_a = hop(from_left[:, :half], "mp", 1)
    far_b = hop(from_right[:, half:], "mp", -1)
    own = ring(own, 3)
    sides = project([from_left, from_right], head_weight, value_weight)
    sides, own[5:7], far_a, far_b = lax.optimization_barrier((sides, own[5:7], far_a, far_b))
    sides, own = ring(sides, 1), ring(own)
    far = [[project([far_a, far_b], head_weight, value_weight)]]
    sides[1:3], far = lax.optimization_barrier((sides[1:3], far))
    sides, far = ring(sides, 2), ring(far, 1)
    wanted = after((owner_shard * entries + entry_slot).reshape(-1), sides[1:3])
    plane_wanted = lax.all_gather(wanted, ("y", "c"), axis=0, tiled=False)
    sides[3:5], far[1:3], own[7], plane_wanted = lax.optimization_barrier(
        (sides[3:5], far[1:3], own[7], plane_wanted)
    )
    sides, far = ring(sides, 3), ring(far, 2)
    sides[5:7], far[3:5] = lax.optimization_barrier((sides[5:7], far[3:5]))

    deltas = jnp.array(DELTAS, jnp.int32)
    shards = (y * NZ + (z + deltas) % NZ) * NC + c
    match = (plane_wanted // entries)[None] == shards[:, None, None]
    asks = jnp.arange(wanted.shape[0], dtype=jnp.int32)
    used = jnp.any(match, axis=2).astype(jnp.int32).reshape(-1)
    seg_at = jnp.sum(jnp.where(match, asks // 2, 0), axis=2).reshape(-1)
    entry_at = jnp.sum(jnp.where(match, (plane_wanted % entries)[None], 0), axis=2).reshape(-1)
    tables = (seg_at, entry_at, used)

    def served(number):
        return attend(CHUNKS[number], tables, qkv, [sum(p, []) for p in zip(own, sides, far)])

    def back(share):
        return lax.all_to_all(share, ("y", "c"), split_axis=0, concat_axis=0, tiled=True)

    first = served(0)
    sides, far = ring(sides, 4), ring(far, 3)
    backs = [back(first)]
    tables = after(tables, first)
    second = served(1)
    sides[7], far[5:7], second = lax.optimization_barrier((sides[7], far[5:7], second))
    far = ring(far, 4)
    backs.append(back(after(second, backs[0])))
    tables = after(tables, backs[0])
    backs.append(back(after(served(2), backs[1])))
    backs.append(back(after(served(3), backs[2])))

    owner = owner_shard.reshape(-1)
    delta = (owner // NC % NZ - z) % NZ
    slot = jnp.where(delta < NZ // 2, 2 * delta, 2 * (NZ - delta) - 1)
    src = owner // (NC * NZ) * NC + owner % NC
    return combine(backs, src, slot)


def solution(mesh):
    grid = Mesh(mesh.devices.reshape(NY, NZ, NC, -1), ("y", "z", "c", "mp"))
    group = ("y", "z", "c")
    in_specs = (
        P(group, "mp", None),
        P(None, "mp"),
        P(None, "mp"),
        P(group, "mp"),
        P(group, "mp"),
        P(group, "mp"),
        P(group, None),
        P(group, None),
    )
    return jax.shard_map(
        per_device, mesh=grid, in_specs=in_specs, out_specs=P(group, "mp"), check_vma=False
    )
```

time: 658 us -> 292 us (0.44)
  waiting for transfers between devices: 452 us -> 90.7 us
  Pallas kernels: 0 us -> 67.9 us
  local copies, waits for them, and re-layouts: 74.1 us -> 12.3 us
  matrix products: 47.6 us -> 0 us
  starting transfers between devices: 51.9 us -> 78.9 us
  blocking collectives: 0 us -> 16.3 us
  other arithmetic: 17.9 us -> 6.5 us
    all_to_all x7 -> x4, waiting for transfers between devices: 451 us -> 19.1 us  [back(): lax.all_to_all(share, ('y', 'c'), split_axis=0, concat_axis=0, tiled=True)]
    ppermute x0 -> x28, waiting for transfers between devices: none -> 71.6 us  [hop(): return lax.ppermute(x, axis, [(i, (i + step) % n) for i in range(n)])]
    pallas_call x0 -> x8, Pallas kernels: none -> 67.9 us  [the longest x4 35.9 us: attend(): pl.pallas_call(functools.partial(attend_kernel, slots, [len(held[slot]) f...]
    ppermute x0 -> x28, starting transfers between devices: none -> 55.6 us  [hop(): return lax.ppermute(x, axis, [(i, (i + step) % n) for i in range(n)])]
    dot_general x4 -> x0, matrix products: 47.6 us -> none  [the longest x1 21.9 us: partial_attend(): jnp.einsum('...htn,...nhd->...thd', exponent, value_matrix_rows.astype(jn...]
    all_to_all x7 -> x4, starting transfers between devices: 51.9 us -> 23.4 us  [back(): lax.all_to_all(share, ('y', 'c'), split_axis=0, concat_axis=0, tiled=True)]
    gather x8 -> x0, local copies, waits for them, and re-layouts: 23.6 us -> none  [the longest x1 7.22 us: per_device(): projected[lax.all_to_all(entry_at, 'group', split_axis=0, concat_axis=0,...]
    another operation x3 -> x0, local copies, waits for them, and re-layouts: 20.8 us -> none
  transfers between devices with their start and end apart: 8 -> 33, of which waited for: 6 -> 16; matrix products, arithmetic and copies ran while one was open for 11% -> 5% of each run, Pallas kernels for 0% -> 17%
where the time goes in v1:
time: 292 us; the launch traced here: 287 us
  waiting for transfers between devices  90.7 us (31%)
  starting transfers between devices  78.9 us (27%)
  Pallas kernels  67.9 us (23%)
  blocking collectives  16.3 us (6%)
  between operations  14.6 us (5%)
  local copies, waits for them, and re-layouts  12.3 us (4%)
  other arithmetic  6.5 us (2%)
    ppermute x28, waiting for transfers between devices, hop(): return lax.ppermute(x, axis, [(i, (i + step) % n) for i in range(n)])  71.6 us
    ppermute x28, starting transfers between devices, hop(): return lax.ppermute(x, axis, [(i, (i + step) % n) for i in range(n)])  55.6 us
    pallas_call x4, Pallas kernels, attend(): pl.pallas_call(functools.partial(attend_kernel, slots, [len(held[slot]) f...  35.9 us
    pallas_call x3, Pallas kernels, project(): pl.pallas_call(kernel, in_specs=[pl.BlockSpec(memory_space=pl.ANY)] * (n...  24.3 us
    all_to_all x4, starting transfers between devices, back(): lax.all_to_all(share, ('y', 'c'), split_axis=0, concat_axis=0, tiled=True)  23.4 us
    all_to_all x4, waiting for transfers between devices, back(): lax.all_to_all(share, ('y', 'c'), split_axis=0, concat_axis=0, tiled=True)  19.1 us
    unnamed x1, blocking collectives  16.3 us
    pallas_call x1, Pallas kernels, combine(): pl.pallas_call(combine_kernel, in_specs=[pl.BlockSpec(memory_space=pltpu....  7.72 us
  transfers between devices with their start and end apart: 33, of which 16 were waited for; matrix products, arithmetic and copies ran while one was open for 5% of the time, Pallas kernels for 17%

profile of v1, /device:TPU:1, one launch (start us, length us, event | category | flops | bytes accessed | tf_op | source)
XLA Modules:
  0.0 287.3 jit_solution(11784125057436008782)
XLA Ops:
  6.5 3.3 %pad_maximum_fusion = bf16[832,1536]{1,0:T(8,128)(2,1)} fusion(bf16[832,512]{1,0:T(8,128)(2,1)} %param.14, bf16[832,512]{1,0:T(8,128)(2,1)} %param.13, bf16[832,512]{1,0:T(8,128)(2,1)} %param.12), kind=kLoop, calls=%fused_computation | loop fusion | flops 7667712 | bytes 5111808 | tf_op jit(solution)/shard_map/concatenate | solution.py:295
  13.4 6.9 %project.3.refs_6_.refs_7_ = bf16[6,32,1024]{2,1,0:T(8,128)(2,1)} custom-call(bf16[6,32,4096]{2,1,0:T(8,128)(2,1)} %refs_0_.1, bf16[4096,512]{1,0:T(8,128)(2,1)} %refs_2_.5, bf16[4096,512]{1,0:T(8,128)(2,1)} %refs_3_.3), custom_call_target="tpu_custom_call" | custom-call | flops 1610612736 | bytes 10354688 | tf_op jit(solution)/shard_map/project/pallas_call | solution.py:73
  22.1 4.0 %collective-permute-start.2 = (bf16[6,32,1024]{2,1,0:T(8,128)(2,1)}, bf16[6,32,1024]{2,1,0:T(8,128)(2,1)S(1)}, u32[]{:S(2)}, u32[]{:S(2)}) collective-permute-start(bf16[6,32,1024]{2,1,0:T(8,128)(2,1)} %project.3.refs_6_.refs_7_), channel_id=1, source_target_pairs={{0,56},{8,0},{16,8},{24,16},{32,24},{40,32},{48,40},{56,48},{1,57}... | collective-permute-start | bytes 1179656 | tf_op jit(solution)/shard_map/ppermute | solution.py:259
  26.2 8.4 %collective-permute-done.refs_12_.refs_13_ = bf16[6,32,1024]{2,1,0:T(8,128)(2,1)S(1)} collective-permute-done((bf16[6,32,1024]{2,1,0:T(8,128)(2,1)}, bf16[6,32,1024]{2,1,0:T(8,128)(2,1)S(1)}, u32[]{:S(2)}, u32[]{:S(2)}) %collective-permute-start) | collective-permute-done | bytes 393248 | tf_op jit(solution)/shard_map/ppermute | solution.py:259
  34.6 2.7 collective-permute-start.3
  37.3 7.5 %collective-permute-done.1.refs_4_.refs_5_ = bf16[6,32,1024]{2,1,0:T(8,128)(2,1)} collective-permute-done((bf16[6,32,1024]{2,1,0:T(8,128)(2,1)S(1)}, bf16[6,32,1024]{2,1,0:T(8,128)(2,1)}, u32[]{:S(2)}, u32[]{:S(2)}) %collective-permute-start.1) | collective-permute-done | bytes 393248 | tf_op jit(solution)/shard_map/ppermute | solution.py:259
  51.6 2.4 collective-permute-start.6
  54.0 3.9 %collective-permute-start.7 = (bf16[6,32,1024]{2,1,0:T(8,128)(2,1)}, bf16[6,32,1024]{2,1,0:T(8,128)(2,1)S(1)}, u32[]{:S(2)}, u32[]{:S(2)}) collective-permute-start(bf16[6,32,1024]{2,1,0:T(8,128)(2,1)} %collective-permute-done.3.refs_10_.refs_11_), channel_id=1, source_target_pairs={{0,56},{8,0},{16,8},{24,16},{32,24},{40,32},{48,40},{56,48},{1,57}... | collective-permute-start | bytes 1179656 | tf_op jit(solution)/shard_map/ppermute | solution.py:259
  57.9 9.4 %project.4.refs_8_.refs_9_ = bf16[6,64,1024]{2,1,0:T(8,128)(2,1)} custom-call(bf16[6,32,4096]{2,1,0:T(8,128)(2,1)} %copy-done.5, bf16[6,32,4096]{2,1,0:T(8,128)(2,1)} %copy-done.6, bf16[4096,512]{1,0:T(8,128)(2,1)} %refs_2_.5, bf16[4096,512]{1,0:T(8,128)(2,1)} %refs_3_.3), custom_call_target="tpu_custom_call" | custom-call | flops 3221225472 | bytes 12320768 | tf_op jit(solution)/shard_map/project/pallas_call | solution.py:73
  69.7 4.1 %collective-permute-start.11 = (bf16[6,64,1024]{2,1,0:T(8,128)(2,1)}, bf16[6,64,1024]{2,1,0:T(8,128)(2,1)S(1)}, u32[]{:S(2)}, u32[]{:S(2)}) collective-permute-start(bf16[6,64,1024]{2,1,0:T(8,128)(2,1)} %project.4.refs_8_.refs_9_), channel_id=1, source_target_pairs={{0,56},{8,0},{16,8},{24,16},{32,24},{40,32},{48,40},{56,48},{1,57}... | collective-permute-start | bytes 2359304 | tf_op jit(solution)/shard_map/ppermute | solution.py:259
  73.8 8.0 %project.5.refs_10_.refs_11_ = bf16[6,32,1024]{2,1,0:T(8,128)(2,1)} custom-call(bf16[6,16,4096]{2,1,0:T(8,128)(2,1)} %collective-permute-done.8.refs_0_, bf16[6,16,4096]{2,1,0:T(8,128)(2,1)} %collective-permute-done.9.refs_1_, bf16[4096,512]{1,0:T(8,128)(2,1)} %refs_2_.5, bf16[4096,512]{1,0:T(8,128)(2,1)} %refs_3_.3), custom_call_target="tpu_custom_call" | custom-call | flops 1610612736 | bytes 10354688 | tf_op jit(solution)/shard_map/project/pallas_call | solution.py:73
  81.8 7.1 %collective-permute-done.10.refs_14_.refs_15_ = bf16[6,64,1024]{2,1,0:T(8,128)(2,1)S(1)} collective-permute-done((bf16[6,64,1024]{2,1,0:T(8,128)(2,1)}, bf16[6,64,1024]{2,1,0:T(8,128)(2,1)S(1)}, u32[]{:S(2)}, u32[]{:S(2)}) %collective-permute-start.10) | collective-permute-done | bytes 786464 | tf_op jit(solution)/shard_map/ppermute | solution.py:259
  89.0 2.7 collective-permute-start.13
  98.6 11.5 %collective-permute-done.16.refs_2_.refs_3_ = bf16[6,16,1024]{2,1,0:T(8,128)(2,1)S(1)} collective-permute-done((bf16[6,16,1024]{2,1,0:T(8,128)(2,1)}, bf16[6,16,1024]{2,1,0:T(8,128)(2,1)S(1)}, u32[]{:S(2)}, u32[]{:S(2)}) %collective-permute-start.16) | collective-permute-done | bytes 196640 | tf_op jit(solution)/shard_map/ppermute | solution.py:259
  111.9 16.3 %all-reduce = s32[208]{0:T(256)S(1)} all-reduce(s32[208]{0:T(256)S(1)} %dynamic-update-slice), channel_id=2, replica_groups=mesh['y'=4,'z'=8,'c'=2,'mp'=4] {'y','c'}, use_global_device_ids=true, to_apply=%add | all-reduce | flops 208 | bytes 1664
  131.6 10.3 %attend.4 = bf16[8,64,1664]{2,1,0:T(8,128)(2,1)} custom-call(s32[64]{0:T(128)} %reshape.24.seg_at, s32[64]{0:T(128)} %reshape.25.entry_at, s32[64]{0:T(128)} %reshape.27.used_at, bf16[104,64,1536]{2,1,0:T(8,128)(2,1)} %bitcast.2, bf16[104,64,1536]{2,1,0:T(8,128)(2,1)} %bitcast.3, bf16[104,64,1536]{2,1,0:T(8,128)(2,1)} %bitcast.4, ...), custom_call_target="tpu_custom_call" | custom-call | flops 1048576 | bytes 1048576 | tf_op jit(solution)/shard_map/attend/pallas_call | solution.py:190
  141.9 6.5 %all-to-all-start = ((bf16[8,64,1664]{2,1,0:T(8,128)(2,1)}), bf16[8,64,1664]{2,1,0:T(8,128)(2,1)S(1)}, u32[]{:S(2)}, u32[]{:S(2)}) async-start(bf16[8,64,1664]{2,1,0:T(8,128)(2,1)} %attend.4), calls=%async_computation | async-start | bytes 3407872 | tf_op jit(solution)/shard_map/all_to_all | solution.py:332
  148.5 9.2 %collective-permute-start.18 = (bf16[6,64,1024]{2,1,0:T(8,128)(2,1)}, bf16[6,64,1024]{2,1,0:T(8,128)(2,1)S(1)}, u32[]{:S(2)}, u32[]{:S(2)}) collective-permute-start(bf16[6,64,1024]{2,1,0:T(8,128)(2,1)} %collective-permute-done.12.refs_6_.refs_7_), channel_id=1, source_target_pairs={{0,8},{8,16},{16,24},{24,32},{32,40},{40,48},{48,56},{56,0},{1,9},... | collective-permute-start | bytes 2359304 | tf_op jit(solution)/shard_map/ppermute | solution.py:259
  162.6 23.7 %collective-permute-done.20.refs_8_.refs_9_ = bf16[6,32,1024]{2,1,0:T(8,128)(2,1)} collective-permute-done((bf16[6,32,1024]{2,1,0:T(8,128)(2,1)}, bf16[6,32,1024]{2,1,0:T(8,128)(2,1)}, u32[]{:S(2)}, u32[]{:S(2)}) %collective-permute-start.20) | collective-permute-done | bytes 393248 | tf_op jit(solution)/shard_map/ppermute | solution.py:259
  191.2 2.5 collective-permute-start.24
  193.9 11.8 %attend.5 = bf16[8,64,1152]{2,1,0:T(8,128)(2,1)} custom-call(s32[64]{0:T(128)} %reshape.24.seg_at, s32[64]{0:T(128)} %reshape.25.entry_at, s32[64]{0:T(128)} %reshape.27.used_at, bf16[104,64,1536]{2,1,0:T(8,128)(2,1)} %bitcast.8, bf16[104,64,1536]{2,1,0:T(8,128)(2,1)} %bitcast.9, bf16[104,64,1536]{2,1,0:T(8,128)(2,1)} %bitcast.10, ...), custom_call_target="tpu_custom_call" | custom-call | flops 1048576 | bytes 1048576 | tf_op jit(solution)/shard_map/attend/pallas_call | solution.py:190
  208.3 2.7 collective-permute-done.25.refs_14_.refs_15_
  210.9 5.7 %all-to-all-start.1 = ((bf16[8,64,1152]{2,1,0:T(8,128)(2,1)}), bf16[8,64,1152]{2,1,0:T(8,128)(2,1)S(1)}, u32[]{:S(2)}, u32[]{:S(2)}) async-start(bf16[8,64,1152]{2,1,0:T(8,128)(2,1)} %attend.5), calls=%async_computation.1 | async-start | bytes 2359296 | tf_op jit(solution)/shard_map/all_to_all | solution.py:332
  216.6 8.3 %attend.6 = bf16[8,64,1152]{2,1,0:T(8,128)(2,1)} custom-call(s32[64]{0:T(128)} %reshape.24.seg_at, s32[64]{0:T(128)} %reshape.25.entry_at, s32[64]{0:T(128)} %reshape.27.used_at, bf16[104,64,1536]{2,1,0:T(8,128)(2,1)} %bitcast.12, bf16[104,64,1536]{2,1,0:T(8,128)(2,1)} %bitcast.13, bf16[104,64,1536]{2,1,0:T(8,128)(2,1)} %bitcast.14, ...), custom_call_target="tpu_custom_call" | custom-call | flops 1048576 | bytes 1048576 | tf_op jit(solution)/shard_map/attend/pallas_call | solution.py:190
  225.0 8.2 %all-to-all-done.1.refs_1_ = bf16[8,64,1152]{2,1,0:T(8,128)(2,1)S(1)} async-done(((bf16[8,64,1152]{2,1,0:T(8,128)(2,1)}), bf16[8,64,1152]{2,1,0:T(8,128)(2,1)S(1)}, u32[]{:S(2)}, u32[]{:S(2)}) %all-to-all-start.1) | async-done | bytes 1179680 | tf_op jit(solution)/shard_map/all_to_all | solution.py:332
  233.1 4.3 %all-to-all-start.2 = ((bf16[8,64,1152]{2,1,0:T(8,128)(2,1)}), bf16[8,64,1152]{2,1,0:T(8,128)(2,1)S(1)}, u32[]{:S(2)}, u32[]{:S(2)}) async-start(bf16[8,64,1152]{2,1,0:T(8,128)(2,1)} %attend.6), calls=%async_computation.2 | async-start | bytes 2359296 | tf_op jit(solution)/shard_map/all_to_all | solution.py:332
  238.5 2.4 collective-permute-start.26
  241.2 4.9 %collective-permute-done.26.refs_10_.refs_11_ = bf16[6,16,1024]{2,1,0:T(8,128)(2,1)S(1)} collective-permute-done((bf16[6,16,1024]{2,1,0:T(8,128)(2,1)S(1)}, bf16[6,16,1024]{2,1,0:T(8,128)(2,1)S(1)}, u32[]{:S(2)}, u32[]{:S(2)}) %collective-permute-start.26) | collective-permute-done | bytes 196640 | tf_op jit(solution)/shard_map/ppermute | solution.py:259
  247.6 5.5 %attend.7 = bf16[8,64,640]{2,1,0:T(8,128)(2,1)} custom-call(s32[64]{0:T(128)} %reshape.24.seg_at, s32[64]{0:T(128)} %reshape.25.entry_at, s32[64]{0:T(128)} %reshape.27.used_at, bf16[104,64,1536]{2,1,0:T(8,128)(2,1)} %bitcast.16, bf16[104,64,1536]{2,1,0:T(8,128)(2,1)} %bitcast.17, bf16[6,16,1024]{2,1,0:T(8,128)(2,1)} %copy-done.18, ...), custom_call_target="tpu_custom_call" | custom-call | flops 1048576 | bytes 1048576 | tf_op jit(solution)/shard_map/attend/pallas_call | solution.py:190
  254.0 6.8 %all-to-all-start.3 = ((bf16[8,64,640]{2,1,0:T(8,128)(2,1)}), bf16[8,64,640]{2,1,0:T(8,128)(2,1)S(1)}, u32[]{:S(2)}, u32[]{:S(2)}) async-start(bf16[8,64,640]{2,1,0:T(8,128)(2,1)} %attend.7), calls=%async_computation.3 | async-start | bytes 1310720 | tf_op jit(solution)/shard_map/all_to_all | solution.py:332
  261.6 10.1 %all-to-all-done.3.refs_3_ = bf16[8,64,640]{2,1,0:T(8,128)(2,1)S(1)} async-done(((bf16[8,64,640]{2,1,0:T(8,128)(2,1)}), bf16[8,64,640]{2,1,0:T(8,128)(2,1)S(1)}, u32[]{:S(2)}, u32[]{:S(2)}) %all-to-all-start.3) | async-done | bytes 655392 | tf_op jit(solution)/shard_map/all_to_all | solution.py:332
  272.5 7.7 %combine.1 = bf16[832,512]{1,0:T(8,128)(2,1)} custom-call(s32[26]{0:T(128)} %get-tuple-element.86.src, s32[26]{0:T(128)} %get-tuple-element.85.slot, bf16[8,64,1664]{2,1,0:T(8,128)(2,1)} %copy-done, bf16[8,64,1152]{2,1,0:T(8,128)(2,1)} %copy-done.3, bf16[8,64,1152]{2,1,0:T(8,128)(2,1)} %copy-done.4, bf16[8,64,640]{2,1,0:T(8,128)(2,1)} %copy-done.10), custom_call_target="tpu_custom_call" | custom-call | tf_op jit(solution)/shard_map/combine/pallas_call | solution.py:246
  (122 shorter events, 43.6 us)
Async XLA Ops:
  6.5 125.1 %all-gather.3.cloned.1.call-start = ((), (), s32[]{:S(2)}) async-start(), calls=%async_computation.4 | async-start | bytes 23003136 | tf_op jit(solution)/shard_map/all_gather | solution.py:296
  9.9 35.5 %collective-permute-start.4 = (bf16[6,32,4096]{2,1,0:T(8,128)(2,1)}, bf16[6,32,4096]{2,1,0:T(8,128)(2,1)S(1)}, u32[]{:S(2)}, u32[]{:S(2)}) collective-permute-start(bf16[6,32,4096]{2,1,0:T(8,128)(2,1)} %refs_0_.1), channel_id=1, source_target_pairs={{0,1},{1,2},{2,3},{3,0},{4,5},{5,6},{6,7},{7,4},{8,9},{9,10},{10,1... | collective-permute-start | bytes 4718600 | tf_op jit(solution)/shard_map/ppermute | solution.py:259
  12.0 34.9 %collective-permute-start.5 = (bf16[6,32,4096]{2,1,0:T(8,128)(2,1)}, bf16[6,32,4096]{2,1,0:T(8,128)(2,1)S(1)}, u32[]{:S(2)}, u32[]{:S(2)}) collective-permute-start(bf16[6,32,4096]{2,1,0:T(8,128)(2,1)} %refs_0_.1), channel_id=1, source_target_pairs={{0,3},{1,0},{2,1},{3,2},{4,7},{5,4},{6,5},{7,6},{8,11},{9,8},{10,9... | collective-permute-start | bytes 4718600 | tf_op jit(solution)/shard_map/ppermute | solution.py:259
  20.3 14.3 %collective-permute-start = (bf16[6,32,1024]{2,1,0:T(8,128)(2,1)}, bf16[6,32,1024]{2,1,0:T(8,128)(2,1)S(1)}, u32[]{:S(2)}, u32[]{:S(2)}) collective-permute-start(bf16[6,32,1024]{2,1,0:T(8,128)(2,1)} %project.3.refs_6_.refs_7_), channel_id=1, source_target_pairs={{0,8},{8,16},{16,24},{24,32},{32,40},{40,48},{48,56},{56,0},{1,9},... | collective-permute-start | bytes 1179656 | tf_op jit(solution)/shard_map/ppermute | solution.py:259
  22.1 12.5 %collective-permute-start.2 = (bf16[6,32,1024]{2,1,0:T(8,128)(2,1)}, bf16[6,32,1024]{2,1,0:T(8,128)(2,1)S(1)}, u32[]{:S(2)}, u32[]{:S(2)}) collective-permute-start(bf16[6,32,1024]{2,1,0:T(8,128)(2,1)} %project.3.refs_6_.refs_7_), channel_id=1, source_target_pairs={{0,56},{8,0},{16,8},{24,16},{32,24},{40,32},{48,40},{56,48},{1,57}... | collective-permute-start | bytes 1179656 | tf_op jit(solution)/shard_map/ppermute | solution.py:259
  34.6 10.2 %collective-permute-start.1 = (bf16[6,32,1024]{2,1,0:T(8,128)(2,1)S(1)}, bf16[6,32,1024]{2,1,0:T(8,128)(2,1)}, u32[]{:S(2)}, u32[]{:S(2)}) collective-permute-start(bf16[6,32,1024]{2,1,0:T(8,128)(2,1)S(1)} %collective-permute-done.refs_12_.refs_13_), channel_id=1, source_target_pairs={{0,8},{8,16},{16,24},{24,32},{32,40},{40,48},{48,56},{56,0},{1,9},... | collective-permute-start | bytes 1179656 | tf_op jit(solution)/shard_map/ppermute | solution.py:259
  34.6 10.2 %collective-permute-start.3 = (bf16[6,32,1024]{2,1,0:T(8,128)(2,1)S(1)}, bf16[6,32,1024]{2,1,0:T(8,128)(2,1)}, u32[]{:S(2)}, u32[]{:S(2)}) collective-permute-start(bf16[6,32,1024]{2,1,0:T(8,128)(2,1)S(1)} %collective-permute-done.2.refs_18_.refs_19_), channel_id=1, source_target_pairs={{0,56},{8,0},{16,8},{24,16},{32,24},{40,32},{48,40},{56,48},{1,57}... | collective-permute-start | bytes 1179656 | tf_op jit(solution)/shard_map/ppermute | solution.py:259
  47.9 19.5 %collective-permute-start.8 = (bf16[6,16,4096]{2,1,0:T(8,128)(2,1)}, bf16[6,16,4096]{2,1,0:T(8,128)(2,1)}, u32[]{:S(2)}, u32[]{:S(2)}) collective-permute-start(bf16[6,16,4096]{2,1,0:T(8,128)(2,1)} %slice.24), channel_id=1, source_target_pairs={{0,1},{1,2},{2,3},{3,0},{4,5},{5,6},{6,7},{7,4},{8,9},{9,10},{10,1... | collective-permute-start | bytes 2359304 | tf_op jit(solution)/shard_map/ppermute | solution.py:259
  50.5 17.3 %collective-permute-start.9 = (bf16[6,16,4096]{2,1,0:T(8,128)(2,1)}, bf16[6,16,4096]{2,1,0:T(8,128)(2,1)}, u32[]{:S(2)}, u32[]{:S(2)}) collective-permute-start(bf16[6,16,4096]{2,1,0:T(8,128)(2,1)} %slice.25), channel_id=1, source_target_pairs={{0,3},{1,0},{2,1},{3,2},{4,7},{5,4},{6,5},{7,6},{8,11},{9,8},{10,9... | collective-permute-start | bytes 2359304 | tf_op jit(solution)/shard_map/ppermute | solution.py:259
  51.6 15.8 %collective-permute-start.6 = (bf16[6,32,1024]{2,1,0:T(8,128)(2,1)}, bf16[6,32,1024]{2,1,0:T(8,128)(2,1)S(1)}, u32[]{:S(2)}, u32[]{:S(2)}) collective-permute-start(bf16[6,32,1024]{2,1,0:T(8,128)(2,1)} %collective-permute-done.1.refs_4_.refs_5_), channel_id=1, source_target_pairs={{0,8},{8,16},{16,24},{24,32},{32,40},{40,48},{48,56},{56,0},{1,9},... | collective-permute-start | bytes 1179656 | tf_op jit(solution)/shard_map/ppermute | solution.py:259
  54.0 13.4 %collective-permute-start.7 = (bf16[6,32,1024]{2,1,0:T(8,128)(2,1)}, bf16[6,32,1024]{2,1,0:T(8,128)(2,1)S(1)}, u32[]{:S(2)}, u32[]{:S(2)}) collective-permute-start(bf16[6,32,1024]{2,1,0:T(8,128)(2,1)} %collective-permute-done.3.refs_10_.refs_11_), channel_id=1, source_target_pairs={{0,56},{8,0},{16,8},{24,16},{32,24},{40,32},{48,40},{56,48},{1,57}... | collective-permute-start | bytes 1179656 | tf_op jit(solution)/shard_map/ppermute | solution.py:259
  67.8 21.1 %collective-permute-start.10 = (bf16[6,64,1024]{2,1,0:T(8,128)(2,1)}, bf16[6,64,1024]{2,1,0:T(8,128)(2,1)S(1)}, u32[]{:S(2)}, u32[]{:S(2)}) collective-permute-start(bf16[6,64,1024]{2,1,0:T(8,128)(2,1)} %project.4.refs_8_.refs_9_), channel_id=1, source_target_pairs={{0,8},{8,16},{16,24},{24,32},{32,40},{40,48},{48,56},{56,0},{1,9},... | collective-permute-start | bytes 2359304 | tf_op jit(solution)/shard_map/ppermute | solution.py:259
  69.7 19.2 %collective-permute-start.11 = (bf16[6,64,1024]{2,1,0:T(8,128)(2,1)}, bf16[6,64,1024]{2,1,0:T(8,128)(2,1)S(1)}, u32[]{:S(2)}, u32[]{:S(2)}) collective-permute-start(bf16[6,64,1024]{2,1,0:T(8,128)(2,1)} %project.4.refs_8_.refs_9_), channel_id=1, source_target_pairs={{0,56},{8,0},{16,8},{24,16},{32,24},{40,32},{48,40},{56,48},{1,57}... | collective-permute-start | bytes 2359304 | tf_op jit(solution)/shard_map/ppermute | solution.py:259
  88.9 39.4 %collective-permute-start.12 = (bf16[6,64,1024]{2,1,0:T(8,128)(2,1)S(1)}, bf16[6,64,1024]{2,1,0:T(8,128)(2,1)}, u32[]{:S(2)}, u32[]{:S(2)}) collective-permute-start(bf16[6,64,1024]{2,1,0:T(8,128)(2,1)S(1)} %collective-permute-done.10.refs_14_.refs_15_), channel_id=1, source_target_pairs={{0,8},{8,16},{16,24},{24,32},{32,40},{40,48},{48,56},{56,0},{1,9},... | collective-permute-start | bytes 2359304 | tf_op jit(solution)/shard_map/ppermute | solution.py:259
  89.0 39.4 %collective-permute-start.13 = (bf16[6,64,1024]{2,1,0:T(8,128)(2,1)S(1)}, bf16[6,64,1024]{2,1,0:T(8,128)(2,1)S(1)}, u32[]{:S(2)}, u32[]{:S(2)}) collective-permute-start(bf16[6,64,1024]{2,1,0:T(8,128)(2,1)S(1)} %collective-permute-done.11.refs_20_.refs_21_), channel_id=1, source_target_pairs={{0,56},{8,0},{16,8},{24,16},{32,24},{40,32},{48,40},{56,48},{1,57}... | collective-permute-start | bytes 2359304 | tf_op jit(solution)/shard_map/ppermute | solution.py:259
  92.4 17.7 %collective-permute-start.16 = (bf16[6,16,1024]{2,1,0:T(8,128)(2,1)}, bf16[6,16,1024]{2,1,0:T(8,128)(2,1)S(1)}, u32[]{:S(2)}, u32[]{:S(2)}) collective-permute-start(bf16[6,16,1024]{2,1,0:T(8,128)(2,1)} %slice.26), channel_id=1, source_target_pairs={{0,8},{8,16},{16,24},{24,32},{32,40},{40,48},{48,56},{56,0},{1,9},... | collective-permute-start | bytes 589832 | tf_op jit(solution)/shard_map/ppermute | solution.py:259
  92.4 35.9 %collective-permute-start.14 = (bf16[6,32,1024]{2,1,0:T(8,128)(2,1)}, bf16[6,32,1024]{2,1,0:T(8,128)(2,1)S(1)}, u32[]{:S(2)}, u32[]{:S(2)}) collective-permute-start(bf16[6,32,1024]{2,1,0:T(8,128)(2,1)} %project.5.refs_10_.refs_11_), channel_id=1, source_target_pairs={{0,8},{8,16},{16,24},{24,32},{32,40},{40,48},{48,56},{56,0},{1,9},... | collective-permute-start | bytes 1179656 | tf_op jit(solution)/shard_map/ppermute | solution.py:259
  93.9 34.4 %collective-permute-start.15 = (bf16[6,32,1024]{2,1,0:T(8,128)(2,1)}, bf16[6,32,1024]{2,1,0:T(8,128)(2,1)}, u32[]{:S(2)}, u32[]{:S(2)}) collective-permute-start(bf16[6,32,1024]{2,1,0:T(8,128)(2,1)} %project.5.refs_10_.refs_11_), channel_id=1, source_target_pairs={{0,56},{8,0},{16,8},{24,16},{32,24},{40,32},{48,40},{56,48},{1,57}... | collective-permute-start | bytes 1179656 | tf_op jit(solution)/shard_map/ppermute | solution.py:259
  110.1 18.2 %collective-permute-start.17 = (bf16[6,16,1024]{2,1,0:T(8,128)(2,1)}, bf16[6,16,1024]{2,1,0:T(8,128)(2,1)S(1)}, u32[]{:S(2)}, u32[]{:S(2)}) collective-permute-start(bf16[6,16,1024]{2,1,0:T(8,128)(2,1)} %slice.27), channel_id=1, source_target_pairs={{0,56},{8,0},{16,8},{24,16},{32,24},{40,32},{48,40},{56,48},{1,57}... | collective-permute-start | bytes 589832 | tf_op jit(solution)/shard_map/ppermute | solution.py:259
  141.9 69.0 %all-to-all-start = ((bf16[8,64,1664]{2,1,0:T(8,128)(2,1)}), bf16[8,64,1664]{2,1,0:T(8,128)(2,1)S(1)}, u32[]{:S(2)}, u32[]{:S(2)}) async-start(bf16[8,64,1664]{2,1,0:T(8,128)(2,1)} %attend.4), calls=%async_computation | async-start | bytes 3407872 | tf_op jit(solution)/shard_map/all_to_all | solution.py:332
  148.5 38.4 %collective-permute-start.18 = (bf16[6,64,1024]{2,1,0:T(8,128)(2,1)}, bf16[6,64,1024]{2,1,0:T(8,128)(2,1)S(1)}, u32[]{:S(2)}, u32[]{:S(2)}) collective-permute-start(bf16[6,64,1024]{2,1,0:T(8,128)(2,1)} %collective-permute-done.12.refs_6_.refs_7_), channel_id=1, source_target_pairs={{0,8},{8,16},{16,24},{24,32},{32,40},{40,48},{48,56},{56,0},{1,9},... | collective-permute-start | bytes 2359304 | tf_op jit(solution)/shard_map/ppermute | solution.py:259
  157.7 29.2 %collective-permute-start.19 = (bf16[6,64,1024]{2,1,0:T(8,128)(2,1)}, bf16[6,64,1024]{2,1,0:T(8,128)(2,1)S(1)}, u32[]{:S(2)}, u32[]{:S(2)}) collective-permute-start(bf16[6,64,1024]{2,1,0:T(8,128)(2,1)} %copy-done.7), channel_id=1, source_target_pairs={{0,56},{8,0},{16,8},{24,16},{32,24},{40,32},{48,40},{56,48},{1,57}... | collective-permute-start | bytes 2359304 | tf_op jit(solution)/shard_map/ppermute | solution.py:259
  159.9 26.4 %collective-permute-start.20 = (bf16[6,32,1024]{2,1,0:T(8,128)(2,1)}, bf16[6,32,1024]{2,1,0:T(8,128)(2,1)}, u32[]{:S(2)}, u32[]{:S(2)}) collective-permute-start(bf16[6,32,1024]{2,1,0:T(8,128)(2,1)} %copy-done.17), channel_id=1, source_target_pairs={{0,8},{8,16},{16,24},{24,32},{32,40},{40,48},{48,56},{56,0},{1,9},... | collective-permute-start | bytes 1179656 | tf_op jit(solution)/shard_map/ppermute | solution.py:259
  160.5 26.4 %collective-permute-start.21 = (bf16[6,32,1024]{2,1,0:T(8,128)(2,1)}, bf16[6,32,1024]{2,1,0:T(8,128)(2,1)}, u32[]{:S(2)}, u32[]{:S(2)}) collective-permute-start(bf16[6,32,1024]{2,1,0:T(8,128)(2,1)} %collective-permute-done.15.refs_22_.refs_23_), channel_id=1, source_target_pairs={{0,56},{8,0},{16,8},{24,16},{32,24},{40,32},{48,40},{56,48},{1,57}... | collective-permute-start | bytes 1179656 | tf_op jit(solution)/shard_map/ppermute | solution.py:259
  187.8 17.9 %collective-permute-start.22 = (bf16[6,32,1024]{2,1,0:T(8,128)(2,1)}, bf16[6,32,1024]{2,1,0:T(8,128)(2,1)}, u32[]{:S(2)}, u32[]{:S(2)}) collective-permute-start(bf16[6,32,1024]{2,1,0:T(8,128)(2,1)} %slice.28), channel_id=1, source_target_pairs={{0,8},{8,16},{16,24},{24,32},{32,40},{40,48},{48,56},{56,0},{1,9},... | collective-permute-start | bytes 1179656 | tf_op jit(solution)/shard_map/ppermute | solution.py:259
  190.9 14.9 %collective-permute-start.23 = (bf16[6,32,1024]{2,1,0:T(8,128)(2,1)}, bf16[6,32,1024]{2,1,0:T(8,128)(2,1)}, u32[]{:S(2)}, u32[]{:S(2)}) collective-permute-start(bf16[6,32,1024]{2,1,0:T(8,128)(2,1)} %slice.29), channel_id=1, source_target_pairs={{0,56},{8,0},{16,8},{24,16},{32,24},{40,32},{48,40},{56,48},{1,57}... | collective-permute-start | bytes 1179656 | tf_op jit(solution)/shard_map/ppermute | solution.py:259
  191.2 16.3 %collective-permute-start.24 = (bf16[6,32,1024]{2,1,0:T(8,128)(2,1)}, bf16[6,32,1024]{2,1,0:T(8,128)(2,1)S(1)}, u32[]{:S(2)}, u32[]{:S(2)}) collective-permute-start(bf16[6,32,1024]{2,1,0:T(8,128)(2,1)} %collective-permute-done.20.refs_8_.refs_9_), channel_id=1, source_target_pairs={{0,8},{8,16},{16,24},{24,32},{32,40},{40,48},{48,56},{56,0},{1,9},... | collective-permute-start | bytes 1179656 | tf_op jit(solution)/shard_map/ppermute | solution.py:259
  193.8 17.1 %collective-permute-start.25 = (bf16[6,32,1024]{2,1,0:T(8,128)(2,1)}, bf16[6,32,1024]{2,1,0:T(8,128)(2,1)}, u32[]{:S(2)}, u32[]{:S(2)}) collective-permute-start(bf16[6,32,1024]{2,1,0:T(8,128)(2,1)} %collective-permute-done.21.refs_14_.refs_15_), channel_id=1, source_target_pairs={{0,56},{8,0},{16,8},{24,16},{32,24},{40,32},{48,40},{56,48},{1,57}... | collective-permute-start | bytes 1179656 | tf_op jit(solution)/shard_map/ppermute | solution.py:259
  210.9 22.2 %all-to-all-start.1 = ((bf16[8,64,1152]{2,1,0:T(8,128)(2,1)}), bf16[8,64,1152]{2,1,0:T(8,128)(2,1)S(1)}, u32[]{:S(2)}, u32[]{:S(2)}) async-start(bf16[8,64,1152]{2,1,0:T(8,128)(2,1)} %attend.5), calls=%async_computation.1 | async-start | bytes 2359296 | tf_op jit(solution)/shard_map/all_to_all | solution.py:332
  233.1 20.9 %all-to-all-start.2 = ((bf16[8,64,1152]{2,1,0:T(8,128)(2,1)}), bf16[8,64,1152]{2,1,0:T(8,128)(2,1)S(1)}, u32[]{:S(2)}, u32[]{:S(2)}) async-start(bf16[8,64,1152]{2,1,0:T(8,128)(2,1)} %attend.6), calls=%async_computation.2 | async-start | bytes 2359296 | tf_op jit(solution)/shard_map/all_to_all | solution.py:332
  238.5 7.7 %collective-permute-start.26 = (bf16[6,16,1024]{2,1,0:T(8,128)(2,1)S(1)}, bf16[6,16,1024]{2,1,0:T(8,128)(2,1)S(1)}, u32[]{:S(2)}, u32[]{:S(2)}) collective-permute-start(bf16[6,16,1024]{2,1,0:T(8,128)(2,1)S(1)} %slice.30), channel_id=1, source_target_pairs={{0,8},{8,16},{16,24},{24,32},{32,40},{40,48},{48,56},{56,0},{1,9},... | collective-permute-start | bytes 589832 | tf_op jit(solution)/shard_map/ppermute | solution.py:259
  254.0 17.7 %all-to-all-start.3 = ((bf16[8,64,640]{2,1,0:T(8,128)(2,1)}), bf16[8,64,640]{2,1,0:T(8,128)(2,1)S(1)}, u32[]{:S(2)}, u32[]{:S(2)}) async-start(bf16[8,64,640]{2,1,0:T(8,128)(2,1)} %attend.7), calls=%async_computation.3 | async-start | bytes 1310720 | tf_op jit(solution)/shard_map/all_to_all | solution.py:332
  (26 other events, 444.7 us)
Sparse Core Ops, SparseCore 0:
  10.0 107.1 all-gather.2
